TPU v7x, 512 devices: a whole 4x8x8 slice. The times are simulated.
512 devices in a mesh: tm: 4 (over x), space: 128 (over z, y, core).
Axes of the slice: x: 4, y: 8, z: 8, core: 2. Of those that a mesh axis runs over, the one named last changes fastest.
Arguments:
- q_start: float32 [5, 512, 64, 128], P(None, 'space'), may hold values from -3.6 to 3.6
- guess: float32 [4, 5, 512, 64, 128], P('tm', None, 'space'), may hold values from -3.6 to 3.6
Outputs:
- corrected: float32 [4, 5, 512, 64, 128], P('tm', None, 'space')
- residual: float32 [4, 5, 512, 64, 128], P('tm', None, 'space')
All inputs are finite; a program needn't handle non-finite values.
Results may differ from a plain program's by a relative error of at most 0.00011.
Values sent between devices are 32-bit elements; how exact they have to be, the bound alone decides.
No kernel may reach another device: no remote copies, remote signals or barrier semaphores. Data moves between devices by JAX's collectives and lax.ppermute only.
A program may use at most 64 MiB of HBM per device.

v0:
```python
import jax
import jax.numpy as jnp
from jax import lax
from jax.sharding import PartitionSpec as P

NZ = 128
COMP = 5
STEPS_SLAB = 2
SWEEPS = 2
BLK = 4
time_step = 0.1
cross = 8.0
axial = 2.0
linear_rate = 0.1
quadratic_rate = 0.5
cubic_rate = 1.0


def with_halo(block, sides, width):
    for axis, dim in sides:
        count = lax.axis_size(axis)
        forward = [(i, i + 1) for i in range(count - 1)]
        backward = [(target, source) for source, target in forward]
        low = lax.ppermute(
            lax.slice_in_dim(block, block.shape[dim] - width, None, axis=dim), axis, forward
        )
        high = lax.ppermute(lax.slice_in_dim(block, 0, width, axis=dim), axis, backward)
        block = jnp.concatenate([low, block, high], axis=dim)
    return block


def passed_along(block, axis, distance):
    devices = range(lax.axis_size(axis))
    route = [(i - distance, i) for i in devices if i - distance in devices]
    return lax.ppermute(block, axis, route)


def prefix(part, axis, combine, identity):
    place = lax.axis_index(axis)
    gathered = jax.tree.map(lambda a: lax.all_gather(a, axis), part)
    state = jax.tree.map(lambda a, e: jnp.zeros_like(a) + jnp.asarray(e, a.dtype), part, identity)

    def one(turn, state):
        return combine(
            state, jax.tree.map(lambda a: lax.dynamic_index_in_dim(a, turn, 0, False), gathered)
        )

    return lax.fori_loop(0, place, one, state)


def bulk_terms(field):
    first, second, third, fourth, fifth = (field[0], field[1], field[2], field[3], field[4])
    sixth = -first - fourth
    s_aa = first * first + second * second + third * third
    s_ab = first * second + second * fourth + third * fifth
    s_ac = first * third + second * fifth + third * sixth
    s_bb = second * second + fourth * fourth + fifth * fifth
    s_bc = second * third + fourth * fifth + fifth * sixth
    trace = (
        first * first
        + fourth * fourth
        + sixth * sixth
        + 2.0 * (second * second + third * third + fifth * fifth)
    )
    quad = jnp.stack([s_aa - trace / 3.0, s_ab, s_ac, s_bb - trace / 3.0, s_bc])
    source = field + time_step * quadratic_rate * quad
    diagonal = 1.0 + time_step * (linear_rate + cubic_rate * trace) + 2.0 * (2.0 * cross + axial)
    return (source, diagonal)


def jacobi(extended, source, diagonal):
    inner = extended[:, 1:-1]
    along_x = extended[:, :-2] + extended[:, 2:]
    padded_y = jnp.pad(inner, ((0, 0), (0, 0), (1, 1), (0, 0)))
    along_y = padded_y[:, :, :-2] + padded_y[:, :, 2:]
    along_z = jnp.roll(inner, 1, 3) + jnp.roll(inner, -1, 3)
    return (source + cross * (along_x + along_y) + axial * along_z) / diagonal[None]


def extend(field, margin):
    return with_halo(field, (("space", 1),), margin)


def propagate(field):
    for step in range(STEPS_SLAB):
        source, diagonal = bulk_terms(field)
        current = field
        for sweep in range(SWEEPS):
            current = jacobi(extend(current, 1), source, diagonal)
        field = current
    return field


def chain_combine(earlier, later):
    return (earlier[0] * later[0], later[0] * earlier[1] + later[1])


def per_device(q_start, guess):
    own = guess[0]
    position = lax.axis_index("tm")
    prior = passed_along(own, "tm", 1)
    start = jnp.where(position == 0, q_start, prior)
    relaxed = propagate(start)
    moved = passed_along(relaxed, "tm", 1)
    start_two = jnp.where(position == 0, q_start, moved)
    again = propagate(start_two)
    residual = again - relaxed
    change = again - own
    cells_total = change.shape[1] * change.shape[2] * lax.axis_size("space")
    partial_sum = jnp.sum(change, axis=(1, 2))
    partial_sum = partial_sum.reshape(COMP, NZ // BLK, BLK).sum(axis=2)
    totals = lax.psum(partial_sum, "space")
    coarse = totals / (cells_total * BLK)
    decay = 1.0 / (1.0 + STEPS_SLAB * time_step * linear_rate)
    factor = jnp.full((), decay, jnp.float32)
    identity = (jnp.ones((), jnp.float32), jnp.zeros_like(coarse))
    passed = prefix((factor, coarse), "tm", chain_combine, identity)
    error = decay * passed[1] + coarse
    spread = jnp.broadcast_to(error[:, None, None, :, None], (COMP, 1, 1, NZ // BLK, BLK))
    spread = spread.reshape(COMP, 1, 1, NZ)
    corrected = relaxed + spread
    return (corrected[None], residual[None])


def solution(mesh):
    return jax.shard_map(
        per_device,
        mesh=mesh,
        in_specs=(P(None, "space", None, None), P("tm", None, "space", None, None)),
        out_specs=(P("tm", None, "space", None, None), P("tm", None, "space", None, None)),
        check_vma=False,
    )
```

profile of v0, /device:TPU:262, one launch (start us, length us, event | category | flops | bytes accessed | tf_op | source)
XLA Modules:
  0.0 409.1 jit_solution(18188361148212606499)
XLA Ops:
  1.9 17.3 %collective-permute-done = f32[5,4,64,128]{3,2,1,0:T(8,128)S(1)} collective-permute-done((f32[5,4,64,128]{3,2,1,0:T(8,128)}, f32[5,4,64,128]{3,2,1,0:T(8,128)S(1)}, u32[]{:S(2)}, u32[]{:S(2)}) %collective-permute-start) | collective-permute-done | bytes 655392 | tf_op jit(solution)/shard_map/ppermute | solution.py:35
  20.1 1.9 collective-permute-start.1
  22.0 7.0 %collective-permute-start.2 = (f32[5,1,64,128]{3,2,1,0:T(8,128)S(1)}, f32[5,1,64,128]{3,2,1,0:T(8,128)S(1)}, u32[]{:S(2)}, u32[]{:S(2)}) collective-permute-start(f32[5,1,64,128]{3,2,1,0:T(8,128)S(1)} %get-tuple-element.114), channel_id=1, source_target_pairs={{1,0},{2,1},{3,2},{4,3},{5,4},{6,5},{7,6},{8,7},{9,8},{10,9},{11,1... | collective-permute-start | bytes 491528 | tf_op jit(solution)/shard_map/ppermute | solution.py:27
  30.0 1.8 collective-permute-done.2
  32.7 1.9 collective-permute-start.3
  34.6 7.1 %collective-permute-start.4 = (f32[5,1,64,128]{3,2,1,0:T(8,128)S(1)}, f32[5,1,64,128]{3,2,1,0:T(8,128)S(1)}, u32[]{:S(2)}, u32[]{:S(2)}) collective-permute-start(f32[5,1,64,128]{3,2,1,0:T(8,128)S(1)} %get-tuple-element.108), channel_id=1, source_target_pairs={{1,0},{2,1},{3,2},{4,3},{5,4},{6,5},{7,6},{8,7},{9,8},{10,9},{11,1... | collective-permute-start | bytes 491528 | tf_op jit(solution)/shard_map/ppermute | solution.py:27
  42.8 1.8 collective-permute-done.4
  46.0 1.9 collective-permute-start.5
  47.9 7.1 %collective-permute-start.6 = (f32[5,1,64,128]{3,2,1,0:T(8,128)S(1)}, f32[5,1,64,128]{3,2,1,0:T(8,128)S(1)}, u32[]{:S(2)}, u32[]{:S(2)}) collective-permute-start(f32[5,1,64,128]{3,2,1,0:T(8,128)S(1)} %get-tuple-element.102), channel_id=1, source_target_pairs={{1,0},{2,1},{3,2},{4,3},{5,4},{6,5},{7,6},{8,7},{9,8},{10,9},{11,1... | collective-permute-start | bytes 491528 | tf_op jit(solution)/shard_map/ppermute | solution.py:27
  56.1 1.8 collective-permute-done.6
  58.7 1.9 collective-permute-start.7
  60.7 7.1 %collective-permute-start.8 = (f32[5,1,64,128]{3,2,1,0:T(8,128)S(1)}, f32[5,1,64,128]{3,2,1,0:T(8,128)S(1)}, u32[]{:S(2)}, u32[]{:S(2)}) collective-permute-start(f32[5,1,64,128]{3,2,1,0:T(8,128)S(1)} %get-tuple-element.96), channel_id=1, source_target_pairs={{1,0},{2,1},{3,2},{4,3},{5,4},{6,5},{7,6},{8,7},{9,8},{10,9},{11,1... | collective-permute-start | bytes 491528 | tf_op jit(solution)/shard_map/ppermute | solution.py:27
  74.6 11.7 %all-reduce.8 = f32[4]{0:T(128)S(1)} all-reduce(f32[4]{0:T(128)S(1)} %dynamic-update-slice), channel_id=1, replica_groups=mesh['tm'=4,'space'=128] {'tm'}, use_global_device_ids=true, to_apply=%add.8 | all-reduce | flops 4 | bytes 32
  87.1 1.9 collective-permute-start.10
  89.1 7.9 %collective-permute-start.11 = (f32[5,1,64,128]{3,2,1,0:T(8,128)S(1)}, f32[5,1,64,128]{3,2,1,0:T(8,128)S(1)}, u32[]{:S(2)}, u32[]{:S(2)}) collective-permute-start(f32[5,1,64,128]{3,2,1,0:T(8,128)S(1)} %get-tuple-element.90), channel_id=1, source_target_pairs={{1,0},{2,1},{3,2},{4,3},{5,4},{6,5},{7,6},{8,7},{9,8},{10,9},{11,1... | collective-permute-start | bytes 491528 | tf_op jit(solution)/shard_map/ppermute | solution.py:27
  100.7 1.9 collective-permute-start.12
  102.6 7.1 %collective-permute-start.13 = (f32[5,1,64,128]{3,2,1,0:T(8,128)S(1)}, f32[5,1,64,128]{3,2,1,0:T(8,128)S(1)}, u32[]{:S(2)}, u32[]{:S(2)}) collective-permute-start(f32[5,1,64,128]{3,2,1,0:T(8,128)S(1)} %get-tuple-element.84), channel_id=1, source_target_pairs={{1,0},{2,1},{3,2},{4,3},{5,4},{6,5},{7,6},{8,7},{9,8},{10,9},{11,1... | collective-permute-start | bytes 491528 | tf_op jit(solution)/shard_map/ppermute | solution.py:27
  114.0 1.9 collective-permute-start.14
  116.0 7.1 %collective-permute-start.15 = (f32[5,1,64,128]{3,2,1,0:T(8,128)S(1)}, f32[5,1,64,128]{3,2,1,0:T(8,128)S(1)}, u32[]{:S(2)}, u32[]{:S(2)}) collective-permute-start(f32[5,1,64,128]{3,2,1,0:T(8,128)S(1)} %get-tuple-element.78), channel_id=1, source_target_pairs={{1,0},{2,1},{3,2},{4,3},{5,4},{6,5},{7,6},{8,7},{9,8},{10,9},{11,1... | collective-permute-start | bytes 491528 | tf_op jit(solution)/shard_map/ppermute | solution.py:27
  126.8 1.9 collective-permute-start.16
  128.7 7.1 %collective-permute-start.17 = (f32[5,1,64,128]{3,2,1,0:T(8,128)S(1)}, f32[5,1,64,128]{3,2,1,0:T(8,128)S(1)}, u32[]{:S(2)}, u32[]{:S(2)}) collective-permute-start(f32[5,1,64,128]{3,2,1,0:T(8,128)S(1)} %get-tuple-element.68), channel_id=1, source_target_pairs={{1,0},{2,1},{3,2},{4,3},{5,4},{6,5},{7,6},{8,7},{9,8},{10,9},{11,1... | collective-permute-start | bytes 491528 | tf_op jit(solution)/shard_map/ppermute | solution.py:27
  140.5 252.0 %psum.7 = f32[5,32]{1,0:T(8,128)S(1)} all-reduce(f32[5,32]{1,0:T(8,128)S(1)} %reduce_sum.19), channel_id=1, replica_groups=mesh['tm'=4,'space'=128] {'space'}, use_global_device_ids=true, to_apply=%region_2.3 | all-reduce | flops 160 | bytes 1280 | tf_op jit(solution)/shard_map/psum | solution.py:112
  392.6 11.9 %all-gather.1 = f32[4,5,32]{2,1,0:T(8,128)S(1)} all-gather(f32[1,5,32]{2,1,0:T(8,128)S(1)} %multiply_bitcast_fusion), channel_id=2, replica_groups=mesh['tm'=4,'space'=128] {'tm'}, dimensions={0}, use_global_device_ids=true | all-gather | bytes 3200 | tf_op jit(solution)/shard_map/all_gather | solution.py:40
  404.5 3.5 while.12
  (96 shorter events, 36.7 us)
Async XLA Ops:
  0.6 18.6 %collective-permute-start = (f32[5,4,64,128]{3,2,1,0:T(8,128)}, f32[5,4,64,128]{3,2,1,0:T(8,128)S(1)}, u32[]{:S(2)}, u32[]{:S(2)}) collective-permute-start(f32[5,4,64,128]{3,2,1,0:T(8,128)} %bitcast.24), channel_id=1, source_target_pairs={{0,128},{128,256},{256,384},{1,129},{129,257},{257,385},{2,130},{1... | collective-permute-start | bytes 1966088 | tf_op jit(solution)/shard_map/ppermute | solution.py:35
  20.1 10.0 %collective-permute-start.1 = (f32[5,1,64,128]{3,2,1,0:T(8,128)S(1)}, f32[5,1,64,128]{3,2,1,0:T(8,128)S(1)}, u32[]{:S(2)}, u32[]{:S(2)}) collective-permute-start(f32[5,1,64,128]{3,2,1,0:T(8,128)S(1)} %get-tuple-element.113), channel_id=1, source_target_pairs={{0,1},{1,2},{2,3},{3,4},{4,5},{5,6},{6,7},{7,8},{8,9},{9,10},{10,1... | collective-permute-start | bytes 491528 | tf_op jit(solution)/shard_map/ppermute | solution.py:24
  22.0 9.8 %collective-permute-start.2 = (f32[5,1,64,128]{3,2,1,0:T(8,128)S(1)}, f32[5,1,64,128]{3,2,1,0:T(8,128)S(1)}, u32[]{:S(2)}, u32[]{:S(2)}) collective-permute-start(f32[5,1,64,128]{3,2,1,0:T(8,128)S(1)} %get-tuple-element.114), channel_id=1, source_target_pairs={{1,0},{2,1},{3,2},{4,3},{5,4},{6,5},{7,6},{8,7},{9,8},{10,9},{11,1... | collective-permute-start | bytes 491528 | tf_op jit(solution)/shard_map/ppermute | solution.py:27
  32.7 10.1 %collective-permute-start.3 = (f32[5,1,64,128]{3,2,1,0:T(8,128)S(1)}, f32[5,1,64,128]{3,2,1,0:T(8,128)S(1)}, u32[]{:S(2)}, u32[]{:S(2)}) collective-permute-start(f32[5,1,64,128]{3,2,1,0:T(8,128)S(1)} %get-tuple-element.107), channel_id=1, source_target_pairs={{0,1},{1,2},{2,3},{3,4},{4,5},{5,6},{6,7},{7,8},{8,9},{9,10},{10,1... | collective-permute-start | bytes 491528 | tf_op jit(solution)/shard_map/ppermute | solution.py:24
  34.6 10.0 %collective-permute-start.4 = (f32[5,1,64,128]{3,2,1,0:T(8,128)S(1)}, f32[5,1,64,128]{3,2,1,0:T(8,128)S(1)}, u32[]{:S(2)}, u32[]{:S(2)}) collective-permute-start(f32[5,1,64,128]{3,2,1,0:T(8,128)S(1)} %get-tuple-element.108), channel_id=1, source_target_pairs={{1,0},{2,1},{3,2},{4,3},{5,4},{6,5},{7,6},{8,7},{9,8},{10,9},{11,1... | collective-permute-start | bytes 491528 | tf_op jit(solution)/shard_map/ppermute | solution.py:27
  46.0 10.1 %collective-permute-start.5 = (f32[5,1,64,128]{3,2,1,0:T(8,128)S(1)}, f32[5,1,64,128]{3,2,1,0:T(8,128)S(1)}, u32[]{:S(2)}, u32[]{:S(2)}) collective-permute-start(f32[5,1,64,128]{3,2,1,0:T(8,128)S(1)} %get-tuple-element.101), channel_id=1, source_target_pairs={{0,1},{1,2},{2,3},{3,4},{4,5},{5,6},{6,7},{7,8},{8,9},{9,10},{10,1... | collective-permute-start | bytes 491528 | tf_op jit(solution)/shard_map/ppermute | solution.py:24
  47.9 10.0 %collective-permute-start.6 = (f32[5,1,64,128]{3,2,1,0:T(8,128)S(1)}, f32[5,1,64,128]{3,2,1,0:T(8,128)S(1)}, u32[]{:S(2)}, u32[]{:S(2)}) collective-permute-start(f32[5,1,64,128]{3,2,1,0:T(8,128)S(1)} %get-tuple-element.102), channel_id=1, source_target_pairs={{1,0},{2,1},{3,2},{4,3},{5,4},{6,5},{7,6},{8,7},{9,8},{10,9},{11,1... | collective-permute-start | bytes 491528 | tf_op jit(solution)/shard_map/ppermute | solution.py:27
  58.7 10.1 %collective-permute-start.7 = (f32[5,1,64,128]{3,2,1,0:T(8,128)S(1)}, f32[5,1,64,128]{3,2,1,0:T(8,128)S(1)}, u32[]{:S(2)}, u32[]{:S(2)}) collective-permute-start(f32[5,1,64,128]{3,2,1,0:T(8,128)S(1)} %get-tuple-element.95), channel_id=1, source_target_pairs={{0,1},{1,2},{2,3},{3,4},{4,5},{5,6},{6,7},{7,8},{8,9},{9,10},{10,1... | collective-permute-start | bytes 491528 | tf_op jit(solution)/shard_map/ppermute | solution.py:24
  60.7 10.0 %collective-permute-start.8 = (f32[5,1,64,128]{3,2,1,0:T(8,128)S(1)}, f32[5,1,64,128]{3,2,1,0:T(8,128)S(1)}, u32[]{:S(2)}, u32[]{:S(2)}) collective-permute-start(f32[5,1,64,128]{3,2,1,0:T(8,128)S(1)} %get-tuple-element.96), channel_id=1, source_target_pairs={{1,0},{2,1},{3,2},{4,3},{5,4},{6,5},{7,6},{8,7},{9,8},{10,9},{11,1... | collective-permute-start | bytes 491528 | tf_op jit(solution)/shard_map/ppermute | solution.py:27
  70.6 15.6 %copy-start = (f32[5,4,64,128]{3,2,1,0:T(8,128)S(1)}, f32[5,4,64,128]{3,2,1,0:T(8,128)}, u32[]{:S(2)}) copy-start(f32[5,4,64,128]{3,2,1,0:T(8,128)} %param.4) | copy-start | bytes 1966084
  71.3 15.0 %collective-permute-start.9 = (f32[5,4,64,128]{3,2,1,0:T(8,128)S(1)}, f32[5,4,64,128]{3,2,1,0:T(8,128)S(1)}, u32[]{:S(2)}, u32[]{:S(2)}) collective-permute-start(f32[5,4,64,128]{3,2,1,0:T(8,128)S(1)} %fusion.23), channel_id=1, source_target_pairs={{0,128},{128,256},{256,384},{1,129},{129,257},{257,385},{2,130},{1... | collective-permute-start | bytes 1966088 | tf_op jit(solution)/shard_map/ppermute | solution.py:35
  87.1 10.9 %collective-permute-start.10 = (f32[5,1,64,128]{3,2,1,0:T(8,128)S(1)}, f32[5,1,64,128]{3,2,1,0:T(8,128)S(1)}, u32[]{:S(2)}, u32[]{:S(2)}) collective-permute-start(f32[5,1,64,128]{3,2,1,0:T(8,128)S(1)} %get-tuple-element.89), channel_id=1, source_target_pairs={{0,1},{1,2},{2,3},{3,4},{4,5},{5,6},{6,7},{7,8},{8,9},{9,10},{10,1... | collective-permute-start | bytes 491528 | tf_op jit(solution)/shard_map/ppermute | solution.py:24
  89.1 10.7 %collective-permute-start.11 = (f32[5,1,64,128]{3,2,1,0:T(8,128)S(1)}, f32[5,1,64,128]{3,2,1,0:T(8,128)S(1)}, u32[]{:S(2)}, u32[]{:S(2)}) collective-permute-start(f32[5,1,64,128]{3,2,1,0:T(8,128)S(1)} %get-tuple-element.90), channel_id=1, source_target_pairs={{1,0},{2,1},{3,2},{4,3},{5,4},{6,5},{7,6},{8,7},{9,8},{10,9},{11,1... | collective-permute-start | bytes 491528 | tf_op jit(solution)/shard_map/ppermute | solution.py:27
  100.7 10.1 %collective-permute-start.12 = (f32[5,1,64,128]{3,2,1,0:T(8,128)S(1)}, f32[5,1,64,128]{3,2,1,0:T(8,128)S(1)}, u32[]{:S(2)}, u32[]{:S(2)}) collective-permute-start(f32[5,1,64,128]{3,2,1,0:T(8,128)S(1)} %get-tuple-element.83), channel_id=1, source_target_pairs={{0,1},{1,2},{2,3},{3,4},{4,5},{5,6},{6,7},{7,8},{8,9},{9,10},{10,1... | collective-permute-start | bytes 491528 | tf_op jit(solution)/shard_map/ppermute | solution.py:24
  102.6 10.0 %collective-permute-start.13 = (f32[5,1,64,128]{3,2,1,0:T(8,128)S(1)}, f32[5,1,64,128]{3,2,1,0:T(8,128)S(1)}, u32[]{:S(2)}, u32[]{:S(2)}) collective-permute-start(f32[5,1,64,128]{3,2,1,0:T(8,128)S(1)} %get-tuple-element.84), channel_id=1, source_target_pairs={{1,0},{2,1},{3,2},{4,3},{5,4},{6,5},{7,6},{8,7},{9,8},{10,9},{11,1... | collective-permute-start | bytes 491528 | tf_op jit(solution)/shard_map/ppermute | solution.py:27
  114.0 10.1 %collective-permute-start.14 = (f32[5,1,64,128]{3,2,1,0:T(8,128)S(1)}, f32[5,1,64,128]{3,2,1,0:T(8,128)S(1)}, u32[]{:S(2)}, u32[]{:S(2)}) collective-permute-start(f32[5,1,64,128]{3,2,1,0:T(8,128)S(1)} %get-tuple-element.77), channel_id=1, source_target_pairs={{0,1},{1,2},{2,3},{3,4},{4,5},{5,6},{6,7},{7,8},{8,9},{9,10},{10,1... | collective-permute-start | bytes 491528 | tf_op jit(solution)/shard_map/ppermute | solution.py:24
  116.0 10.0 %collective-permute-start.15 = (f32[5,1,64,128]{3,2,1,0:T(8,128)S(1)}, f32[5,1,64,128]{3,2,1,0:T(8,128)S(1)}, u32[]{:S(2)}, u32[]{:S(2)}) collective-permute-start(f32[5,1,64,128]{3,2,1,0:T(8,128)S(1)} %get-tuple-element.78), channel_id=1, source_target_pairs={{1,0},{2,1},{3,2},{4,3},{5,4},{6,5},{7,6},{8,7},{9,8},{10,9},{11,1... | collective-permute-start | bytes 491528 | tf_op jit(solution)/shard_map/ppermute | solution.py:27
  126.8 10.1 %collective-permute-start.16 = (f32[5,1,64,128]{3,2,1,0:T(8,128)S(1)}, f32[5,1,64,128]{3,2,1,0:T(8,128)S(1)}, u32[]{:S(2)}, u32[]{:S(2)}) collective-permute-start(f32[5,1,64,128]{3,2,1,0:T(8,128)S(1)} %get-tuple-element.67), channel_id=1, source_target_pairs={{0,1},{1,2},{2,3},{3,4},{4,5},{5,6},{6,7},{7,8},{8,9},{9,10},{10,1... | collective-permute-start | bytes 491528 | tf_op jit(solution)/shard_map/ppermute | solution.py:24
  128.7 10.0 %collective-permute-start.17 = (f32[5,1,64,128]{3,2,1,0:T(8,128)S(1)}, f32[5,1,64,128]{3,2,1,0:T(8,128)S(1)}, u32[]{:S(2)}, u32[]{:S(2)}) collective-permute-start(f32[5,1,64,128]{3,2,1,0:T(8,128)S(1)} %get-tuple-element.68), channel_id=1, source_target_pairs={{1,0},{2,1},{3,2},{4,3},{5,4},{6,5},{7,6},{8,7},{9,8},{10,9},{11,1... | collective-permute-start | bytes 491528 | tf_op jit(solution)/shard_map/ppermute | solution.py:27
  138.7 1.5 copy-start.1
where the time goes:
time: 410 us; the launch traced here: 409 us
  blocking collectives  276 us (67%)
  starting transfers between devices  75.6 us (18%)
  waiting for transfers between devices  38.6 us (9%)
  other arithmetic  9.83 us (2%)
  local copies, waits for them, and re-layouts  8.23 us (2%)
    psum x1, blocking collectives, per_device(): totals = lax.psum(partial_sum, 'space')  252 us
    ppermute x8, starting transfers between devices, with_halo(): lax.ppermute(lax.slice_in_dim(block, 0, width, axis=dim), axis, backward)  57.7 us
    ppermute x2, waiting for transfers between devices, passed_along(): return lax.ppermute(block, axis, route)  17.3 us
    ppermute x8, starting transfers between devices, with_halo(): lax.ppermute(lax.slice_in_dim(block, block.shape[dim] - width, None, axis...  15.4 us
    ppermute x8, waiting for transfers between devices, with_halo(): lax.ppermute(lax.slice_in_dim(block, 0, width, axis=dim), axis, backward)  14 us
    all_gather x1, blocking collectives, prefix(): gathered = jax.tree.map(lambda a: lax.all_gather(a, axis), part)  11.9 us
    unnamed x1, blocking collectives  11.7 us
  transfers between devices with their start and end apart: 18, of which 17 were waited for; matrix products, arithmetic and copies ran while one was open for 1% of the time, Pallas kernels for 0%

commit v1 on v0

--- a/solution.py
+++ b/solution.py
@@ -109,7 +109,7 @@
     cells_total = change.shape[1] * change.shape[2] * lax.axis_size("space")
     partial_sum = jnp.sum(change, axis=(1, 2))
     partial_sum = partial_sum.reshape(COMP, NZ // BLK, BLK).sum(axis=2)
-    totals = lax.psum(partial_sum, "space")
+    totals = jnp.sum(lax.all_gather(partial_sum, "space"), axis=0)
     coarse = totals / (cells_total * BLK)
     decay = 1.0 / (1.0 + STEPS_SLAB * time_step * linear_rate)
     factor = jnp.full((), decay, jnp.float32)

time: 410 us -> 212 us (0.52)
  the two profiles are of different devices: /device:TPU:262 before, /device:TPU:6 now
where the time goes in v1:
time: 212 us
  blocking collectives  100 us (47%)
  starting transfers between devices  54.8 us (26%)
  waiting for transfers between devices  37.5 us (18%)
  other arithmetic  9.97 us (5%)
  local copies, waits for them, and re-layouts  8.23 us (4%)
    all_gather x1, blocking collectives, per_device(): totals = jnp.sum(lax.all_gather(partial_sum, 'space'), axis=0)  74 us
    ppermute x8, starting transfers between devices, with_halo(): lax.ppermute(lax.slice_in_dim(block, block.shape[dim] - width, None, axis...  41.8 us
    ppermute x8, waiting for transfers between devices, with_halo(): lax.ppermute(lax.slice_in_dim(block, 0, width, axis=dim), axis, backward)  20.2 us
    ppermute x2, waiting for transfers between devices, passed_along(): return lax.ppermute(block, axis, route)  17.3 us
    unnamed x1, blocking collectives  14.1 us
    all_gather x1, blocking collectives, prefix(): gathered = jax.tree.map(lambda a: lax.all_gather(a, axis), part)  11.9 us
    ppermute x8, starting transfers between devices, with_halo(): lax.ppermute(lax.slice_in_dim(block, 0, width, axis=dim), axis, backward)  10.3 us
    div x11, other arithmetic, jacobi(): (source + cross * (along_x + along_y) + axial * along_z) / diagonal[None]  4.56 us
  transfers between devices with their start and end apart: 18, of which 9 were waited for; matrix products, arithmetic and copies ran while one was open for 2% of the time, Pallas kernels for 0%

profile of v1, /device:TPU:6, one launch (start us, length us, event | category | flops | bytes accessed | tf_op | source)
XLA Modules:
  0.0 211.7 jit_solution(6931009808789345556)
XLA Ops:
  1.9 17.3 %collective-permute-done = f32[5,4,64,128]{3,2,1,0:T(8,128)S(1)} collective-permute-done((f32[5,4,64,128]{3,2,1,0:T(8,128)}, f32[5,4,64,128]{3,2,1,0:T(8,128)S(1)}, u32[]{:S(2)}, u32[]{:S(2)}) %collective-permute-start) | collective-permute-done | bytes 655392 | tf_op jit(solution)/shard_map/ppermute | solution.py:35
  20.1 1.3 collective-permute-start.1
  21.4 1.3 collective-permute-start.2
  22.8 3.7 %collective-permute-done.2 = f32[5,1,64,128]{3,2,1,0:T(8,128)S(1)} collective-permute-done((f32[5,1,64,128]{3,2,1,0:T(8,128)S(1)}, f32[5,1,64,128]{3,2,1,0:T(8,128)S(1)}, u32[]{:S(2)}, u32[]{:S(2)}) %collective-permute-start.2) | collective-permute-done | bytes 163872 | tf_op jit(solution)/shard_map/ppermute | solution.py:27
  27.4 5.8 %collective-permute-start.3 = (f32[5,1,64,128]{3,2,1,0:T(8,128)S(1)}, f32[5,1,64,128]{3,2,1,0:T(8,128)S(1)}, u32[]{:S(2)}, u32[]{:S(2)}) collective-permute-start(f32[5,1,64,128]{3,2,1,0:T(8,128)S(1)} %get-tuple-element.107), channel_id=1, source_target_pairs={{0,1},{1,2},{2,3},{3,4},{4,5},{5,6},{6,7},{7,8},{8,9},{9,10},{10,1... | collective-permute-start | bytes 491528 | tf_op jit(solution)/shard_map/ppermute | solution.py:24
  34.7 1.7 collective-permute-done.4
  37.9 5.3 %collective-permute-start.5 = (f32[5,1,64,128]{3,2,1,0:T(8,128)S(1)}, f32[5,1,64,128]{3,2,1,0:T(8,128)S(1)}, u32[]{:S(2)}, u32[]{:S(2)}) collective-permute-start(f32[5,1,64,128]{3,2,1,0:T(8,128)S(1)} %get-tuple-element.101), channel_id=1, source_target_pairs={{0,1},{1,2},{2,3},{3,4},{4,5},{5,6},{6,7},{7,8},{8,9},{9,10},{10,1... | collective-permute-start | bytes 491528 | tf_op jit(solution)/shard_map/ppermute | solution.py:24
  43.1 1.3 collective-permute-start.6
  44.5 1.9 collective-permute-done.6
  47.3 5.3 %collective-permute-start.7 = (f32[5,1,64,128]{3,2,1,0:T(8,128)S(1)}, f32[5,1,64,128]{3,2,1,0:T(8,128)S(1)}, u32[]{:S(2)}, u32[]{:S(2)}) collective-permute-start(f32[5,1,64,128]{3,2,1,0:T(8,128)S(1)} %get-tuple-element.95), channel_id=1, source_target_pairs={{0,1},{1,2},{2,3},{3,4},{4,5},{5,6},{6,7},{7,8},{8,9},{9,10},{10,1... | collective-permute-start | bytes 491528 | tf_op jit(solution)/shard_map/ppermute | solution.py:24
  54.1 1.7 collective-permute-done.8
  59.8 14.1 %all-reduce.8 = f32[4]{0:T(128)S(1)} all-reduce(f32[4]{0:T(128)S(1)} %dynamic-update-slice), channel_id=1, replica_groups=mesh['tm'=4,'space'=128] {'tm'}, use_global_device_ids=true, to_apply=%add.8 | all-reduce | flops 4 | bytes 32
  74.8 5.5 %collective-permute-start.10 = (f32[5,1,64,128]{3,2,1,0:T(8,128)S(1)}, f32[5,1,64,128]{3,2,1,0:T(8,128)S(1)}, u32[]{:S(2)}, u32[]{:S(2)}) collective-permute-start(f32[5,1,64,128]{3,2,1,0:T(8,128)S(1)} %get-tuple-element.89), channel_id=1, source_target_pairs={{0,1},{1,2},{2,3},{3,4},{4,5},{5,6},{6,7},{7,8},{8,9},{9,10},{10,1... | collective-permute-start | bytes 491528 | tf_op jit(solution)/shard_map/ppermute | solution.py:24
  81.7 5.7 %collective-permute-done.11 = f32[5,1,64,128]{3,2,1,0:T(8,128)S(1)} collective-permute-done((f32[5,1,64,128]{3,2,1,0:T(8,128)S(1)}, f32[5,1,64,128]{3,2,1,0:T(8,128)S(1)}, u32[]{:S(2)}, u32[]{:S(2)}) %collective-permute-start.11) | collective-permute-done | bytes 163872 | tf_op jit(solution)/shard_map/ppermute | solution.py:27
  88.2 5.8 %collective-permute-start.12 = (f32[5,1,64,128]{3,2,1,0:T(8,128)S(1)}, f32[5,1,64,128]{3,2,1,0:T(8,128)S(1)}, u32[]{:S(2)}, u32[]{:S(2)}) collective-permute-start(f32[5,1,64,128]{3,2,1,0:T(8,128)S(1)} %get-tuple-element.83), channel_id=1, source_target_pairs={{0,1},{1,2},{2,3},{3,4},{4,5},{5,6},{6,7},{7,8},{8,9},{9,10},{10,1... | collective-permute-start | bytes 491528 | tf_op jit(solution)/shard_map/ppermute | solution.py:24
  95.5 1.7 collective-permute-done.13
  98.7 6.5 %collective-permute-start.14 = (f32[5,1,64,128]{3,2,1,0:T(8,128)S(1)}, f32[5,1,64,128]{3,2,1,0:T(8,128)S(1)}, u32[]{:S(2)}, u32[]{:S(2)}) collective-permute-start(f32[5,1,64,128]{3,2,1,0:T(8,128)S(1)} %get-tuple-element.77), channel_id=1, source_target_pairs={{0,1},{1,2},{2,3},{3,4},{4,5},{5,6},{6,7},{7,8},{8,9},{9,10},{10,1... | collective-permute-start | bytes 491528 | tf_op jit(solution)/shard_map/ppermute | solution.py:24
  106.6 1.9 collective-permute-done.15
  109.4 6.5 %collective-permute-start.16 = (f32[5,1,64,128]{3,2,1,0:T(8,128)S(1)}, f32[5,1,64,128]{3,2,1,0:T(8,128)S(1)}, u32[]{:S(2)}, u32[]{:S(2)}) collective-permute-start(f32[5,1,64,128]{3,2,1,0:T(8,128)S(1)} %get-tuple-element.67), channel_id=1, source_target_pairs={{0,1},{1,2},{2,3},{3,4},{4,5},{5,6},{6,7},{7,8},{8,9},{9,10},{10,1... | collective-permute-start | bytes 491528 | tf_op jit(solution)/shard_map/ppermute | solution.py:24
  117.4 1.7 collective-permute-done.17
  119.2 1.5 subtract_bitcast_fusion
  121.0 74.0 %all-gather.2 = f32[128,5,32]{2,1,0:T(8,128)S(1)} all-gather(f32[1,5,32]{2,1,0:T(8,128)S(1)} %bitcast.26), channel_id=2, replica_groups=mesh['tm'=4,'space'=128] {'space'}, dimensions={0}, use_global_device_ids=true | all-gather | bytes 82560 | tf_op jit(solution)/shard_map/all_gather | solution.py:112
  195.1 11.9 %all-gather.3 = f32[4,5,32]{2,1,0:T(8,128)S(1)} all-gather(f32[1,5,32]{2,1,0:T(8,128)S(1)} %multiply_bitcast_fusion), channel_id=3, replica_groups=mesh['tm'=4,'space'=128] {'tm'}, dimensions={0}, use_global_device_ids=true | all-gather | bytes 3200 | tf_op jit(solution)/shard_map/all_gather | solution.py:40
  207.0 3.5 %while.12 = (s32[]{:T(128)}, f32[5,32]{1,0:T(8,128)S(1)}, s32[]{:T(128)}, f32[4]{0:T(128)S(1)}, f32[4,5,32]{2,1,0:T(8,128)S(1)}, /*index=5*/s32[]{:T(128)}, s32[]{:T(128)}, s32[]{:T(128)}) while((s32[]{:T(128)}, f32[5,32]{1,0:T(8,128)S(1)}, s32[]{:T(128)}, f32[4]{0:T(128)S(1)}, f32[4,5,32]{2,1,0:T(8,128)S(1)}, /*index=5*/s32[]{:T(128)}, ...), condition=%wide.region_4.5_spmd, body=%wide.region_3.4_spmd.sunk | while | flops 325 | bytes 2059 | solution.py:48
  (97 shorter events, 27.0 us)
Async XLA Ops:
  0.6 18.6 %collective-permute-start = (f32[5,4,64,128]{3,2,1,0:T(8,128)}, f32[5,4,64,128]{3,2,1,0:T(8,128)S(1)}, u32[]{:S(2)}, u32[]{:S(2)}) collective-permute-start(f32[5,4,64,128]{3,2,1,0:T(8,128)} %bitcast.25), channel_id=1, source_target_pairs={{0,128},{128,256},{256,384},{1,129},{129,257},{257,385},{2,130},{1... | collective-permute-start | bytes 1966088 | tf_op jit(solution)/shard_map/ppermute | solution.py:35
  20.1 2.7 %collective-permute-start.1 = (f32[5,1,64,128]{3,2,1,0:T(8,128)S(1)}, f32[5,1,64,128]{3,2,1,0:T(8,128)S(1)}, u32[]{:S(2)}, u32[]{:S(2)}) collective-permute-start(f32[5,1,64,128]{3,2,1,0:T(8,128)S(1)} %get-tuple-element.113), channel_id=1, source_target_pairs={{0,1},{1,2},{2,3},{3,4},{4,5},{5,6},{6,7},{7,8},{8,9},{9,10},{10,1... | collective-permute-start | bytes 491528 | tf_op jit(solution)/shard_map/ppermute | solution.py:24
  21.4 5.1 %collective-permute-start.2 = (f32[5,1,64,128]{3,2,1,0:T(8,128)S(1)}, f32[5,1,64,128]{3,2,1,0:T(8,128)S(1)}, u32[]{:S(2)}, u32[]{:S(2)}) collective-permute-start(f32[5,1,64,128]{3,2,1,0:T(8,128)S(1)} %get-tuple-element.114), channel_id=1, source_target_pairs={{1,0},{2,1},{3,2},{4,3},{5,4},{6,5},{7,6},{8,7},{9,8},{10,9},{11,1... | collective-permute-start | bytes 491528 | tf_op jit(solution)/shard_map/ppermute | solution.py:27
  27.4 7.3 %collective-permute-start.3 = (f32[5,1,64,128]{3,2,1,0:T(8,128)S(1)}, f32[5,1,64,128]{3,2,1,0:T(8,128)S(1)}, u32[]{:S(2)}, u32[]{:S(2)}) collective-permute-start(f32[5,1,64,128]{3,2,1,0:T(8,128)S(1)} %get-tuple-element.107), channel_id=1, source_target_pairs={{0,1},{1,2},{2,3},{3,4},{4,5},{5,6},{6,7},{7,8},{8,9},{9,10},{10,1... | collective-permute-start | bytes 491528 | tf_op jit(solution)/shard_map/ppermute | solution.py:24
  33.1 3.3 %collective-permute-start.4 = (f32[5,1,64,128]{3,2,1,0:T(8,128)S(1)}, f32[5,1,64,128]{3,2,1,0:T(8,128)S(1)}, u32[]{:S(2)}, u32[]{:S(2)}) collective-permute-start(f32[5,1,64,128]{3,2,1,0:T(8,128)S(1)} %get-tuple-element.108), channel_id=1, source_target_pairs={{1,0},{2,1},{3,2},{4,3},{5,4},{6,5},{7,6},{8,7},{9,8},{10,9},{11,1... | collective-permute-start | bytes 491528 | tf_op jit(solution)/shard_map/ppermute | solution.py:27
  37.9 6.6 %collective-permute-start.5 = (f32[5,1,64,128]{3,2,1,0:T(8,128)S(1)}, f32[5,1,64,128]{3,2,1,0:T(8,128)S(1)}, u32[]{:S(2)}, u32[]{:S(2)}) collective-permute-start(f32[5,1,64,128]{3,2,1,0:T(8,128)S(1)} %get-tuple-element.101), channel_id=1, source_target_pairs={{0,1},{1,2},{2,3},{3,4},{4,5},{5,6},{6,7},{7,8},{8,9},{9,10},{10,1... | collective-permute-start | bytes 491528 | tf_op jit(solution)/shard_map/ppermute | solution.py:24
  43.1 3.3 %collective-permute-start.6 = (f32[5,1,64,128]{3,2,1,0:T(8,128)S(1)}, f32[5,1,64,128]{3,2,1,0:T(8,128)S(1)}, u32[]{:S(2)}, u32[]{:S(2)}) collective-permute-start(f32[5,1,64,128]{3,2,1,0:T(8,128)S(1)} %get-tuple-element.102), channel_id=1, source_target_pairs={{1,0},{2,1},{3,2},{4,3},{5,4},{6,5},{7,6},{8,7},{9,8},{10,9},{11,1... | collective-permute-start | bytes 491528 | tf_op jit(solution)/shard_map/ppermute | solution.py:27
  47.3 6.8 %collective-permute-start.7 = (f32[5,1,64,128]{3,2,1,0:T(8,128)S(1)}, f32[5,1,64,128]{3,2,1,0:T(8,128)S(1)}, u32[]{:S(2)}, u32[]{:S(2)}) collective-permute-start(f32[5,1,64,128]{3,2,1,0:T(8,128)S(1)} %get-tuple-element.95), channel_id=1, source_target_pairs={{0,1},{1,2},{2,3},{3,4},{4,5},{5,6},{6,7},{7,8},{8,9},{9,10},{10,1... | collective-permute-start | bytes 491528 | tf_op jit(solution)/shard_map/ppermute | solution.py:24
  52.6 3.3 %collective-permute-start.8 = (f32[5,1,64,128]{3,2,1,0:T(8,128)S(1)}, f32[5,1,64,128]{3,2,1,0:T(8,128)S(1)}, u32[]{:S(2)}, u32[]{:S(2)}) collective-permute-start(f32[5,1,64,128]{3,2,1,0:T(8,128)S(1)} %get-tuple-element.96), channel_id=1, source_target_pairs={{1,0},{2,1},{3,2},{4,3},{5,4},{6,5},{7,6},{8,7},{9,8},{10,9},{11,1... | collective-permute-start | bytes 491528 | tf_op jit(solution)/shard_map/ppermute | solution.py:27
  55.8 18.0 %copy-start = (f32[5,4,64,128]{3,2,1,0:T(8,128)S(1)}, f32[5,4,64,128]{3,2,1,0:T(8,128)}, u32[]{:S(2)}) copy-start(f32[5,4,64,128]{3,2,1,0:T(8,128)} %param.4) | copy-start | bytes 1966084
  56.5 17.4 %collective-permute-start.9 = (f32[5,4,64,128]{3,2,1,0:T(8,128)S(1)}, f32[5,4,64,128]{3,2,1,0:T(8,128)S(1)}, u32[]{:S(2)}, u32[]{:S(2)}) collective-permute-start(f32[5,4,64,128]{3,2,1,0:T(8,128)S(1)} %fusion.23), channel_id=1, source_target_pairs={{0,128},{128,256},{256,384},{1,129},{129,257},{257,385},{2,130},{1... | collective-permute-start | bytes 1966088 | tf_op jit(solution)/shard_map/ppermute | solution.py:35
  74.8 6.9 %collective-permute-start.10 = (f32[5,1,64,128]{3,2,1,0:T(8,128)S(1)}, f32[5,1,64,128]{3,2,1,0:T(8,128)S(1)}, u32[]{:S(2)}, u32[]{:S(2)}) collective-permute-start(f32[5,1,64,128]{3,2,1,0:T(8,128)S(1)} %get-tuple-element.89), channel_id=1, source_target_pairs={{0,1},{1,2},{2,3},{3,4},{4,5},{5,6},{6,7},{7,8},{8,9},{9,10},{10,1... | collective-permute-start | bytes 491528 | tf_op jit(solution)/shard_map/ppermute | solution.py:24
  80.3 7.0 %collective-permute-start.11 = (f32[5,1,64,128]{3,2,1,0:T(8,128)S(1)}, f32[5,1,64,128]{3,2,1,0:T(8,128)S(1)}, u32[]{:S(2)}, u32[]{:S(2)}) collective-permute-start(f32[5,1,64,128]{3,2,1,0:T(8,128)S(1)} %get-tuple-element.90), channel_id=1, source_target_pairs={{1,0},{2,1},{3,2},{4,3},{5,4},{6,5},{7,6},{8,7},{9,8},{10,9},{11,1... | collective-permute-start | bytes 491528 | tf_op jit(solution)/shard_map/ppermute | solution.py:27
  88.2 7.3 %collective-permute-start.12 = (f32[5,1,64,128]{3,2,1,0:T(8,128)S(1)}, f32[5,1,64,128]{3,2,1,0:T(8,128)S(1)}, u32[]{:S(2)}, u32[]{:S(2)}) collective-permute-start(f32[5,1,64,128]{3,2,1,0:T(8,128)S(1)} %get-tuple-element.83), channel_id=1, source_target_pairs={{0,1},{1,2},{2,3},{3,4},{4,5},{5,6},{6,7},{7,8},{8,9},{9,10},{10,1... | collective-permute-start | bytes 491528 | tf_op jit(solution)/shard_map/ppermute | solution.py:24
  93.9 3.3 %collective-permute-start.13 = (f32[5,1,64,128]{3,2,1,0:T(8,128)S(1)}, f32[5,1,64,128]{3,2,1,0:T(8,128)S(1)}, u32[]{:S(2)}, u32[]{:S(2)}) collective-permute-start(f32[5,1,64,128]{3,2,1,0:T(8,128)S(1)} %get-tuple-element.84), channel_id=1, source_target_pairs={{1,0},{2,1},{3,2},{4,3},{5,4},{6,5},{7,6},{8,7},{9,8},{10,9},{11,1... | collective-permute-start | bytes 491528 | tf_op jit(solution)/shard_map/ppermute | solution.py:27
  98.7 7.8 %collective-permute-start.14 = (f32[5,1,64,128]{3,2,1,0:T(8,128)S(1)}, f32[5,1,64,128]{3,2,1,0:T(8,128)S(1)}, u32[]{:S(2)}, u32[]{:S(2)}) collective-permute-start(f32[5,1,64,128]{3,2,1,0:T(8,128)S(1)} %get-tuple-element.77), channel_id=1, source_target_pairs={{0,1},{1,2},{2,3},{3,4},{4,5},{5,6},{6,7},{7,8},{8,9},{9,10},{10,1... | collective-permute-start | bytes 491528 | tf_op jit(solution)/shard_map/ppermute | solution.py:24
  105.2 3.3 %collective-permute-start.15 = (f32[5,1,64,128]{3,2,1,0:T(8,128)S(1)}, f32[5,1,64,128]{3,2,1,0:T(8,128)S(1)}, u32[]{:S(2)}, u32[]{:S(2)}) collective-permute-start(f32[5,1,64,128]{3,2,1,0:T(8,128)S(1)} %get-tuple-element.78), channel_id=1, source_target_pairs={{1,0},{2,1},{3,2},{4,3},{5,4},{6,5},{7,6},{8,7},{9,8},{10,9},{11,1... | collective-permute-start | bytes 491528 | tf_op jit(solution)/shard_map/ppermute | solution.py:27
  109.4 8.0 %collective-permute-start.16 = (f32[5,1,64,128]{3,2,1,0:T(8,128)S(1)}, f32[5,1,64,128]{3,2,1,0:T(8,128)S(1)}, u32[]{:S(2)}, u32[]{:S(2)}) collective-permute-start(f32[5,1,64,128]{3,2,1,0:T(8,128)S(1)} %get-tuple-element.67), channel_id=1, source_target_pairs={{0,1},{1,2},{2,3},{3,4},{4,5},{5,6},{6,7},{7,8},{8,9},{9,10},{10,1... | collective-permute-start | bytes 491528 | tf_op jit(solution)/shard_map/ppermute | solution.py:24
  115.9 3.3 %collective-permute-start.17 = (f32[5,1,64,128]{3,2,1,0:T(8,128)S(1)}, f32[5,1,64,128]{3,2,1,0:T(8,128)S(1)}, u32[]{:S(2)}, u32[]{:S(2)}) collective-permute-start(f32[5,1,64,128]{3,2,1,0:T(8,128)S(1)} %get-tuple-element.68), channel_id=1, source_target_pairs={{1,0},{2,1},{3,2},{4,3},{5,4},{6,5},{7,6},{8,7},{9,8},{10,9},{11,1... | collective-permute-start | bytes 491528 | tf_op jit(solution)/shard_map/ppermute | solution.py:27
  119.1 1.5 copy-start.1
